TPU v7x, 256 devices: a whole 4x4x8 slice. The times are simulated.
256 devices in a mesh: segment: 8 (over y, core), ctx: 32 (over z, x).
Axes of the slice: x: 4, y: 4, z: 8, core: 2. Of those that a mesh axis runs over, the one named last changes fastest.
Arguments:
- queries: bfloat16 [256, 8192], P(('segment', 'ctx')), may hold values from -9 to 9
- cache: bfloat16 [524288, 2048], P(('segment', 'ctx')), may hold values from -9 to 9
- out_weight: bfloat16 [65536, 8192], P('segment', 'ctx'), may hold values from -2 to 2
- offsets: int32 [8], P('segment'), may hold values from 21845 to 65504, as said below
- starts: int32 [8], P('segment'), may hold values from 0 to 37422, as said below
Outputs:
- advanced: bfloat16 [256, 8192], P('segment', 'ctx')
Inputs may be any that keep to these rules, and one draw needn't show every extreme that they name: `offsets`: each section's slice ends inside its cache; some section's slice ends at its last cache position. A section's document starts no later than its first query; some section's document starts at 0.
All inputs are finite; a program needn't handle non-finite values.
Results may differ from a plain program's by a relative error of at most 0.0054.
Values may be sent and summed in bfloat16 or wider, within the bound.
A program may use at most 192 MiB of HBM per device.

v0:
```python
import jax
import jax.numpy as jnp
from jax import lax
from jax.sharding import PartitionSpec as P

H = 64
KVH = 8
HD = 128


def merged(value, axis, join):
    pieces = jax.tree.map(lambda part: lax.all_gather(part, axis), value)
    head = jax.tree.map(lambda part: part[0], pieces)
    tail = jax.tree.map(lambda part: part[1:], pieces)
    so_far, _ = lax.scan(lambda so_far, slab: (join(so_far, slab), None), head, tail)
    return so_far


def from_behind(value, axis, by):
    devices = lax.axis_size(axis)
    return lax.ppermute(value, axis, [(i, (i + by) % devices) for i in range(devices)])


def block_state(gathered, cache, offset, doc_start, first_position):
    rows = gathered.shape[0]
    span = cache.shape[0]
    group = H // KVH
    positions = first_position + jnp.arange(span, dtype=jnp.int32)
    query_pos = offset + jnp.arange(rows, dtype=jnp.int32)
    visible = ((positions[None, :] >= doc_start) & (positions[None, :] <= query_pos[:, None]))[
        :, None, :
    ]
    score_scale = HD ** (-0.5)

    def per_group(group_index, carry):
        maxima, sums, outputs = carry
        query_part = lax.dynamic_slice_in_dim(
            gathered, group_index * group * HD, group * HD, 1
        ).reshape(rows * group, HD)
        key_part = lax.dynamic_slice_in_dim(cache, group_index * HD, HD, 1)
        value_part = lax.dynamic_slice_in_dim(cache, (KVH + group_index) * HD, HD, 1)
        scores = lax.dot_general(
            query_part, key_part, (((1,), (1,)), ((), ())), preferred_element_type=jnp.float32
        )
        scores = scores.reshape(rows, group, span) * score_scale
        masked = jnp.where(visible, scores, -1e30)
        row_max = jnp.max(masked, axis=-1)
        weights = jnp.where(visible, jnp.exp(masked - row_max[..., None]), 0.0)
        weight_sum = jnp.sum(weights, axis=-1)
        numerator = jnp.dot(
            weights.astype(jnp.bfloat16).reshape(rows * group, span),
            value_part,
            preferred_element_type=jnp.float32,
        )
        normalized = numerator.reshape(rows, group, HD) / jnp.maximum(weight_sum, 1.0)[..., None]
        head_start = group_index * group
        maxima = lax.dynamic_update_slice_in_dim(maxima, row_max, head_start, 1)
        sums = lax.dynamic_update_slice_in_dim(sums, weight_sum, head_start, 1)
        outputs = lax.dynamic_update_slice_in_dim(outputs, normalized, head_start, 1)
        return (maxima, sums, outputs)

    initial = (
        jnp.zeros((rows, H), jnp.float32),
        jnp.zeros((rows, H), jnp.float32),
        jnp.zeros((rows, H, HD), jnp.float32),
    )
    return lax.fori_loop(0, KVH, per_group, initial)


def tile_state(gathered, tile, offset, doc_start, first_position):
    rows = gathered.shape[0]
    span = tile.shape[0]
    hidden_tile = (first_position + span - 1 < doc_start) | (first_position > offset + rows - 1)

    def skipped(unused):
        return (
            jnp.full((rows, H), -1e30, jnp.float32),
            jnp.zeros((rows, H), jnp.float32),
            jnp.zeros((rows, H, HD), jnp.float32),
        )

    def computed(unused):
        return block_state(gathered, tile, offset, doc_start, first_position)

    return lax.cond(hidden_tile, skipped, computed, 0)


def combine_parts(first, second):
    max_first, sum_first, out_first = first
    max_second, sum_second, out_second = second
    joint = jnp.maximum(max_first, max_second)
    factor_first = sum_first * jnp.exp(max_first - joint)
    factor_second = sum_second * jnp.exp(max_second - joint)
    total = factor_first + factor_second
    mixed = (
        factor_first[..., None] * out_first + factor_second[..., None] * out_second
    ) / jnp.maximum(total, 1.0)[..., None]
    return (joint, total, mixed)


def per_device(queries, cache, out_weight, offsets, starts):
    offset = offsets[0]
    doc_start = starts[0]
    gathered = lax.all_gather(queries, "ctx", axis=0, tiled=True)
    span = cache.shape[0]
    half = span // 2
    position = lax.axis_index("ctx")
    own_state = tile_state(gathered, cache[:half], offset, doc_start, position * span)
    other_state = tile_state(gathered, cache[half:], offset, doc_start, position * span + half)
    maxima, sums, outputs = combine_parts(own_state, other_state)
    rows = gathered.shape[0]
    maxima, sums, outputs = merged((maxima, sums, outputs), "ctx", combine_parts)
    attention = outputs.reshape(rows, H * HD).astype(jnp.bfloat16)
    projected = jnp.dot(attention, out_weight, preferred_element_type=jnp.float32)
    return from_behind(projected.astype(jnp.bfloat16), "segment", 1)


def solution(mesh):
    in_specs = (
        P(("segment", "ctx"), None),
        P(("segment", "ctx"), None),
        P("segment", "ctx"),
        P("segment"),
        P("segment"),
    )
    out_specs = P("segment", "ctx")
    return jax.shard_map(
        per_device, mesh=mesh, in_specs=in_specs, out_specs=out_specs, check_vma=False
    )
```

profile of v0, /device:TPU:1, one launch (start us, length us, event | category | flops | bytes accessed | tf_op | source)
XLA Modules:
  0.0 486.7 jit_solution(17538322998228450009)
XLA Ops:
  7.8 43.0 %all-gather.3 = bf16[32,1,8192]{2,1,0:T(2,128)(2,1)S(1)} all-gather(bf16[1,1,8192]{2,1,0:T(2,128)(2,1)} %bitcast.97), channel_id=1, replica_groups=mesh['segment'=8,'ctx'=32] {'ctx'}, dimensions={0}, use_global_device_ids=true | all-gather | bytes 540672 | tf_op jit(solution)/shard_map/all_gather | solution.py:104
  51.5 38.3 %conditional.3 = (f32[32,64]{1,0:T(8,128)S(1)}, f32[32,64]{1,0:T(8,128)S(1)}, f32[32,64,128]{2,1,0:T(8,128)S(1)}) conditional(s32[]{:T(128)} %convert_element_type.36, (bf16[2048,2048]{1,0:T(8,128)(2,1)}, s32[]{:T(128)}, s32[]{:T(128)}, s32[]{:T(128)}, bf16[32,8192]{1,0:T(8,128)(2,1)S(1)}) %tuple.137, () %tuple.72), branch_computations={%region_6.11_spmd, %region_11.12_spmd} | conditional | flops 136678176 | bytes 13766461 | solution.py:85
  52.1 4.7 slice.19
  57.6 32.1 %while.53 = (s32[]{:T(128)}, f32[32,64]{1,0:T(8,128)S(1)}, f32[32,64]{1,0:T(8,128)S(1)}, f32[32,64,128]{2,1,0:T(8,128)S(1)}, bf16[32,8192]{1,0:T(8,128)(2,1)S(1)...) while((s32[]{:T(128)}, f32[32,64]{1,0:T(8,128)S(1)}, ...), condition=%wide.region_10.10_spmd.clone, body=%wide.region_7.9_spmd.clone.sunk | while | flops 136675072 | bytes 4307449 | solution.py:67
  91.8 83.9 %all-gather = f32[1024,64]{1,0:T(8,128)S(1)} all-gather(f32[32,64]{1,0:T(8,128)S(1)} %get-tuple-element.548), channel_id=2, replica_groups=mesh['segment'=8,'ctx'=32] {'ctx'}, dimensions={0}, use_global_device_ids=true | all-gather | bytes 270336 | tf_op jit(solution)/shard_map/all_gather | solution.py:12
  175.7 39.1 %all-gather.1 = f32[1024,64]{1,0:T(8,128)S(1)} all-gather(f32[32,64]{1,0:T(8,128)S(1)} %get-tuple-element.545), channel_id=3, replica_groups=mesh['segment'=8,'ctx'=32] {'ctx'}, dimensions={0}, use_global_device_ids=true | all-gather | bytes 270336 | tf_op jit(solution)/shard_map/all_gather | solution.py:12
  214.9 166.7 %all-gather.6.cloned.1.call-done = f32[1024,64,128]{2,1,0:T(8,128)} async-done(((f32[32,64,128]{2,1,0:T(8,128)}), f32[1024,64,128]{2,1,0:T(8,128)}) %all-gather.6.cloned.1.call-update) | async-done | bytes 33554448 | tf_op jit(solution)/shard_map/all_gather | solution.py:12
  381.6 23.1 %slice.43 = f32[992,64,128]{2,1,0:T(8,128)} slice(f32[1024,64,128]{2,1,0:T(8,128)} %all-gather.6.cloned.1.call-done), slice={[32:1024], [0:64], [0:128]} | slice | bytes 65011712 | tf_op jit(solution)/shard_map/slice | solution.py:14
  404.7 68.0 %while.54 = (s32[]{:T(128)}, f32[32,64]{1,0:T(8,128)S(1)}, f32[32,64]{1,0:T(8,128)S(1)}, f32[32,64,128]{2,1,0:T(8,128)S(1)}, f32[31,32,64]{2,1,0:T(8,128)S(1)}, ...) while((s32[]{:T(128)}, f32[32,64]{1,0:T(8,128)S(1)}, f32[32,64]{1,0:T(8,128)S(1)}, ...), condition=%wide.region_13.14_spmd, body=%wide.region_12.13_spmd.sunk | while | flops 1062914 | bytes 3244125 | solution.py:15
  404.8 2.1 fusion.57
  407.0 2.1 fusion.57
  409.2 2.1 fusion.57
  411.3 2.1 fusion.57
  413.5 2.1 fusion.57
  415.7 2.1 fusion.57
  417.9 2.1 fusion.57
  420.1 2.1 fusion.57
  422.3 2.1 fusion.57
  424.5 2.1 fusion.57
  426.7 2.1 fusion.57
  428.9 2.1 fusion.57
  431.1 2.1 fusion.57
  472.9 3.0 convolution_convert_fusion
  475.9 2.5 collective-permute-start
  (145 shorter events, 76.5 us)
Async XLA Ops:
  6.5 375.1 %all-gather.6.cloned.1.call-start = ((), (), s32[]{:S(2)}) async-start(), calls=%async_computation | async-start | bytes 34603008 | tf_op jit(solution)/shard_map/all_gather | solution.py:12
  381.6 23.1 %slice-start = ((f32[1024,64,128]{2,1,0:T(8,128)}), f32[32,64,128]{2,1,0:T(8,128)S(1)}, s32[]{:S(2)}) async-start(f32[1024,64,128]{2,1,0:T(8,128)} %all-gather.6.cloned.1.call-done), calls=%async_computation.1 | async-start | bytes 2097152 | tf_op jit(solution)/shard_map/slice | solution.py:13
  475.9 3.4 collective-permute-start
Sparse Core Ops, SparseCore 0:
  91.9 289.7 all-gather.5
where the time goes:
time: 489 us; the launch traced here: 487 us
  waiting for transfers between devices  168 us (34%)
  blocking collectives  166 us (34%)
  other arithmetic  74.3 us (15%)
  local copies, waits for them, and re-layouts  34.9 us (7%)
  matrix products  24.9 us (5%)
  between operations  14.8 us (3%)
    all_gather x1, waiting for transfers between devices, merged(): pieces = jax.tree.map(lambda part: lax.all_gather(part, axis), value)  167 us
    all_gather x2, blocking collectives, merged(): pieces = jax.tree.map(lambda part: lax.all_gather(part, axis), value)  123 us
    div x32, other arithmetic, combine_parts(): (factor_first[..., None] * out_first + factor_second[..., None] * out_sec...  68.2 us
    all_gather x1, blocking collectives, per_device(): gathered = lax.all_gather(queries, 'ctx', axis=0, tiled=True)  43 us
    slice x3, local copies, waits for them, and re-layouts, merged(): tail = jax.tree.map(lambda part: part[1:], pieces)  23.2 us
    dot_general x8, matrix products, per_group(): lax.dot_general(query_part, key_part, (((1,), (1,)), ((), ())), preferred...  11.2 us
    dot_general x8, matrix products, per_group(): jnp.dot(weights.astype(jnp.bfloat16).reshape(rows * group, span), value_p...  10.7 us
  transfers between devices with their start and end apart: 2, of which 2 were waited for; matrix products, arithmetic and copies ran while one was open for 0% of the time, Pallas kernels for 0%

commit v1 on v0

v1 whole, which is shorter than its diff:
```python
import functools

import jax
import jax.numpy as jnp
from jax import lax
from jax.experimental import pallas as pl
from jax.experimental.pallas import tpu as pltpu
from jax.sharding import PartitionSpec as P

H = 64
KVH = 8
HD = 128
GROUP = H // KVH
NX = 4
NZ = 8
QS = NX * NZ
ROWS = QS * GROUP
CHUNK = ROWS // NX
SCALE2 = HD ** (-0.5) * 1.4426950408889634
HIDDEN = -1e30
MESH = pl.DeviceIdType.MESH
FAR_FIRST = (4, 3, -3, 2, -2, 1, -1, 0)


def kernel(offsets, starts, q_hbm, cache_hbm, w_hbm, out_ref, qrow, qf, qbuf, qg, fbuf, kbuf, vbuf,
           wbuf, sbuf, pbuf, osend, ostat, xbuf, xstat, zsend, zsstat, zbuf, zstat, abuf, ysend,
           q_load, k_load, v_load, w_load, qz_s, qz_r, qx_s, qx_r, xs_s, xs_r, zs_s, zs_r, az_s,
           az_r, ax_s, ax_r, y_s, y_r):
    segment = lax.axis_index("segment")
    ctx = lax.axis_index("ctx")
    z = ctx // NX
    x = ctx % NX
    n_seg = lax.axis_size("segment")
    span = cache_hbm.shape[0]

    def at_z(step):
        return (z + step + NZ) % NZ

    def at_x(step):
        return (x + step + NX) % NX

    def peer(zz, xx):
        return {"segment": segment, "ctx": zz * NX + xx}

    barrier = pltpu.get_barrier_semaphore()
    for step in range(1, NZ):
        pl.semaphore_signal(barrier, inc=1, device_id=peer(at_z(step), x), device_id_type=MESH)
    for step in range(1, NX):
        pl.semaphore_signal(barrier, inc=1, device_id=peer(z, at_x(step)), device_id_type=MESH)
    before = (segment + n_seg - 1) % n_seg
    after = (segment + 1) % n_seg
    pl.semaphore_signal(
        barrier, inc=1, device_id={"segment": before, "ctx": ctx}, device_id_type=MESH
    )

    q_copy = pltpu.make_async_copy(q_hbm, qrow, q_load)
    q_copy.start()
    k_copies, v_copies = [], []
    for k, dz in enumerate(FAR_FIRST):
        g = at_z(dz)
        k_copies.append(pltpu.make_async_copy(
            cache_hbm.at[:, pl.ds(pl.multiple_of(g * HD, HD), HD)], kbuf.at[k], k_load.at[k]))
        v_copies.append(pltpu.make_async_copy(
            cache_hbm.at[:, pl.ds(pl.multiple_of((KVH + g) * HD, HD), HD)], vbuf.at[k], v_load.at[k]))
        k_copies[k].start()
        v_copies[k].start()
    w_copy = pltpu.make_async_copy(w_hbm, wbuf, w_load)
    w_copy.start()

    q_copy.wait()
    row = qrow[...].astype(jnp.float32)
    for h in range(H):
        qf[h:h + 1, :] = row[:, h * HD:(h + 1) * HD]
    qbuf[ctx] = qf[...].astype(jnp.bfloat16)

    pl.semaphore_wait(barrier, NZ - 1 + NX - 1 + 1)

    def gather(buf, z_send, z_recv, x_send, x_recv, use):
        def along_z(i):
            return pltpu.make_async_remote_copy(
                buf.at[ctx], buf.at[ctx], z_send.at[i], z_recv.at[i],
                device_id=peer(at_z(FAR_FIRST[i]), x), device_id_type=MESH)

        def along_x(i, dx):
            own = at_z(-FAR_FIRST[i]) * NX + x
            return pltpu.make_async_remote_copy(
                buf.at[own], buf.at[own], x_send.at[i, dx - 1], x_recv.at[i, dx - 1],
                device_id=peer(z, at_x(dx)), device_id_type=MESH)

        for i in range(NZ - 1):
            along_z(i).start()
        for dx in range(1, NX):
            along_x(NZ - 1, dx).start()
        use(ctx)
        for i in reversed(range(NZ - 1)):
            along_z(i).wait_recv()
            for dx in range(1, NX):
                along_x(i, dx).start()
            use(at_z(-FAR_FIRST[i]) * NX + x)
        for i in reversed(range(NZ)):
            for dx in range(1, NX):
                along_x(i, dx).wait_recv()
                use(at_z(-FAR_FIRST[i]) * NX + at_x(-dx))

        def finish():
            for i in range(NZ - 1):
                along_z(i).wait_send()
            for i in range(NZ):
                for dx in range(1, NX):
                    along_x(i, dx).wait_send()
        return finish

    offset = offsets[0]
    start = starts[0]
    first = ctx * span
    lanes = lax.broadcasted_iota(jnp.int32, (span // 8, HD), 1)
    for part in range(8):
        position = first + part * (span // 8) + lax.broadcasted_iota(jnp.int32, (span // 8, HD), 0)
        late = jnp.clip(position - offset, 0, QS)
        late = jnp.where(position < start, QS, late)
        fbuf[part * (span // 8):(part + 1) * (span // 8), :] = jnp.where(
            late == lanes, 1.0, 0.0).astype(jnp.bfloat16)
    g_lane = lax.broadcasted_iota(jnp.int32, (ROWS, HD), 1)
    g_row = lax.broadcasted_iota(jnp.int32, (ROWS, HD), 0) % QS
    hide = jnp.where((g_lane > g_row) & (g_lane <= QS), HIDDEN, 0.0).astype(jnp.bfloat16)

    def use_query(c):
        value = qbuf[c].astype(jnp.float32)
        for g in range(KVH):
            qg[g, pl.ds(c, GROUP, stride=QS), :] = value[g * GROUP:(g + 1) * GROUP, :]

    finish_q = gather(qbuf, qz_s, qz_r, qx_s, qx_r, use_query)

    lane = lax.broadcasted_iota(jnp.int32, (CHUNK, HD), 1)
    line = lax.broadcasted_iota(jnp.int32, (CHUNK, HD), 0)
    diagonal = lane == line
    diagonal_high = lane == line + CHUNK
    low = lax.broadcasted_iota(jnp.int32, (1, HD), 1) < CHUNK

    def x_copies(k, dx):
        to = at_x(dx)
        where = peer(z, to)
        return (
            pltpu.make_async_remote_copy(
                osend.at[k, pl.ds(pl.multiple_of(to * CHUNK, CHUNK), CHUNK), :],
                xbuf.at[k, dx - 1], xs_s.at[k, dx - 1, 0], xs_r.at[k, dx - 1, 0],
                device_id=where, device_id_type=MESH),
            pltpu.make_async_remote_copy(
                ostat.at[k, to, pl.ds(0, 1), :], xstat.at[k, dx - 1, pl.ds(0, 1), :],
                xs_s.at[k, dx - 1, 1], xs_r.at[k, dx - 1, 1],
                device_id=where, device_id_type=MESH),
        )

    def z_copies(k, dz):
        where = peer(at_z(dz), x)
        return (
            pltpu.make_async_remote_copy(
                zsend.at[k], zbuf.at[k], zs_s.at[k, 0], zs_r.at[k, 0],
                device_id=where, device_id_type=MESH),
            pltpu.make_async_remote_copy(
                zsstat.at[k, pl.ds(0, 1), :], zstat.at[k, pl.ds(0, 1), :],
                zs_s.at[k, 1], zs_r.at[k, 1], device_id=where, device_id_type=MESH),
        )

    def attend(k, carry):
        pltpu.make_async_copy(
            cache_hbm.at[:, pl.ds(0, HD)], kbuf.at[k], k_load.at[k]).wait()
        pltpu.make_async_copy(
            cache_hbm.at[:, pl.ds(0, HD)], vbuf.at[k], v_load.at[k]).wait()
        magnitude = NZ // 2 - (k + 1) // 2
        g = at_z((2 * (k % 2) - 1) * magnitude)
        query = jnp.concatenate([qg[g].astype(jnp.bfloat16), hide], axis=1)
        tile = 256
        for c in range(span // tile):
            rows = slice(c * tile, (c + 1) * tile)
            keys = jnp.concatenate([kbuf[k, rows, :], fbuf[rows, :]], axis=1)
            sbuf[:, rows] = lax.dot_general(
                query, keys, (((1,), (1,)), ((), ())), preferred_element_type=jnp.float32)
        block = 16
        maxima, sums = [], []
        for r in range(ROWS // block):
            rows = slice(r * block, (r + 1) * block)
            score = sbuf[rows, :]
            top = jnp.max(score, axis=1, keepdims=True)
            weight = jnp.exp2((score - top) * SCALE2)
            maxima.append(jnp.broadcast_to(top * SCALE2, (block, HD)))
            sums.append(jnp.broadcast_to(jnp.sum(weight, axis=1, keepdims=True), (block, HD)))
            pbuf[rows, :] = weight.astype(jnp.bfloat16)
        per = CHUNK // block
        for xx in range(NX):
            top = jnp.concatenate(maxima[xx * per:(xx + 1) * per], axis=0)
            total = jnp.concatenate(sums[xx * per:(xx + 1) * per], axis=0)
            stat = jnp.where(diagonal, top, 0.0) + jnp.where(diagonal_high, total, 0.0)
            ostat[k, xx, 0:1, :] = jnp.sum(stat, axis=0, keepdims=True)
        numerator = jnp.dot(pbuf[...], vbuf[k], preferred_element_type=jnp.float32)
        osend[k] = numerator.astype(jnp.bfloat16)
        for dx in range(1, NX):
            for copy in x_copies(k, dx):
                copy.start()
        return carry

    lax.fori_loop(0, KVH, attend, 0)

    def join(parts):
        stats = [stat for stat, _ in parts]
        top = functools.reduce(jnp.maximum, stats)
        total = jnp.zeros_like(top)
        mixed = jnp.zeros((CHUNK, HD), jnp.float32)
        for stat, numerator in parts:
            factor = jnp.exp2(stat - top)
            total = total + pltpu.roll(factor, CHUNK, 1) * stat
            column = jnp.sum(
                jnp.where(diagonal, jnp.broadcast_to(factor, (CHUNK, HD)), 0.0),
                axis=1, keepdims=True)
            mixed = mixed + column * numerator.astype(jnp.float32)
        return jnp.where(low, top, total), mixed

    own_rows = pl.ds(pl.multiple_of(x * CHUNK, CHUNK), CHUNK)
    for k, dz in enumerate(FAR_FIRST):
        parts = [(ostat[k, x, 0:1, :], osend[k, own_rows, :])]
        for dx in range(1, NX):
            for copy in x_copies(k, dx):
                copy.wait_recv()
            parts.append((xstat[k, dx - 1, 0:1, :], xbuf[k, dx - 1]))
        stat, mixed = join(parts)
        zsend[k] = mixed.astype(jnp.bfloat16)
        zsstat[k, 0:1, :] = stat
        if dz != 0:
            for copy in z_copies(k, dz):
                copy.start()

    own = NZ - 1
    parts = [(zsstat[own, 0:1, :], zsend[own])]
    for k in reversed(range(NZ - 1)):
        for copy in z_copies(k, FAR_FIRST[k]):
            copy.wait_recv()
        parts.append((zstat[k, 0:1, :], zbuf[k]))
    stat, mixed = join(parts)
    divisor = jnp.sum(
        jnp.where(diagonal_high, jnp.broadcast_to(stat, (CHUNK, HD)), 0.0), axis=1, keepdims=True)
    mixed = mixed / divisor
    abuf[ctx] = jnp.concatenate([mixed[:QS], mixed[QS:]], axis=1).astype(jnp.bfloat16)

    w_copy.wait()
    projected = [jnp.zeros((QS, out_ref.shape[1]), jnp.float32)]

    def use_chunk(c):
        projected[0] = projected[0] + jnp.dot(
            abuf[c], wbuf[pl.ds(pl.multiple_of(c * 2 * HD, 2 * HD), 2 * HD), :],
            preferred_element_type=jnp.float32)

    finish_a = gather(abuf, az_s, az_r, ax_s, ax_r, use_chunk)
    ysend[...] = projected[0].astype(jnp.bfloat16)
    y_copy = pltpu.make_async_remote_copy(
        ysend, out_ref, y_s.at[0], y_r.at[0],
        device_id={"segment": after, "ctx": ctx}, device_id_type=MESH)
    y_copy.start()
    finish_q()
    finish_a()
    for k, dz in enumerate(FAR_FIRST):
        for dx in range(1, NX):
            for copy in x_copies(k, dx):
                copy.wait_send()
        if dz != 0:
            for copy in z_copies(k, dz):
                copy.wait_send()
    y_copy.wait()


def per_device(queries, cache, out_weight, offsets, starts):
    span = cache.shape[0]
    columns = out_weight.shape[1]
    bf16, f32 = jnp.bfloat16, jnp.float32
    dma = pltpu.SemaphoreType.DMA
    return pl.pallas_call(
        kernel,
        out_shape=jax.ShapeDtypeStruct((QS, columns), bf16),
        in_specs=[pl.BlockSpec(memory_space=pltpu.SMEM)] * 2 + [pl.BlockSpec(memory_space=pl.ANY)] * 3,
        out_specs=pl.BlockSpec(memory_space=pltpu.VMEM),
        scratch_shapes=[
            pltpu.VMEM((1, H * HD), bf16),
            pltpu.VMEM((H, HD), f32),
            pltpu.VMEM((QS, H, HD), bf16),
            pltpu.VMEM((KVH, ROWS, HD), f32),
            pltpu.VMEM((span, HD), bf16),
            pltpu.VMEM((KVH, span, HD), bf16),
            pltpu.VMEM((KVH, span, HD), bf16),
            pltpu.VMEM((H * HD, columns), bf16),
            pltpu.VMEM((ROWS, span), f32),
            pltpu.VMEM((ROWS, span), bf16),
            pltpu.VMEM((KVH, ROWS, HD), bf16),
            pltpu.VMEM((KVH, NX, 8, HD), f32),
            pltpu.VMEM((KVH, NX - 1, CHUNK, HD), bf16),
            pltpu.VMEM((KVH, NX - 1, 8, HD), f32),
            pltpu.VMEM((NZ, CHUNK, HD), bf16),
            pltpu.VMEM((NZ, 8, HD), f32),
            pltpu.VMEM((NZ, CHUNK, HD), bf16),
            pltpu.VMEM((NZ, 8, HD), f32),
            pltpu.VMEM((QS, QS, 2 * HD), bf16),
            pltpu.VMEM((QS, columns), bf16),
            dma, dma((KVH,)), dma((KVH,)), dma,
            dma((NZ - 1,)), dma((NZ - 1,)), dma((NZ, NX - 1)), dma((NZ, NX - 1)),
            dma((KVH, NX - 1, 2)), dma((KVH, NX - 1, 2)),
            dma((NZ - 1, 2)), dma((NZ - 1, 2)),
            dma((NZ - 1,)), dma((NZ - 1,)), dma((NZ, NX - 1)), dma((NZ, NX - 1)),
            dma((1,)), dma((1,)),
        ],
        compiler_params=pltpu.CompilerParams(collective_id=0, has_side_effects=True),
        name="section_attention",
    )(offsets, starts, queries, cache, out_weight)


def solution(mesh):
    in_specs = (
        P(("segment", "ctx"), None),
        P(("segment", "ctx"), None),
        P("segment", "ctx"),
        P("segment"),
        P("segment"),
    )
    out_specs = P("segment", "ctx")
    return jax.shard_map(
        per_device, mesh=mesh, in_specs=in_specs, out_specs=out_specs, check_vma=False
    )
```

time: 489 us -> 53.7 us (0.11)
  waiting for transfers between devices: 168 us -> 0 us
  blocking collectives: 166 us -> 0 us
  other arithmetic: 74.3 us -> 0 us
  Pallas kernels: 0 us -> 50.9 us
  local copies, waits for them, and re-layouts: 34.9 us -> 1.32 us
  matrix products: 24.9 us -> 0 us
  between operations: 14.8 us -> 1.3 us
    all_gather x1 -> x0, waiting for transfers between devices: 167 us -> none  [merged(): pieces = jax.tree.map(lambda part: lax.all_gather(part, axis), value)]
    all_gather x3 -> x0, blocking collectives: 166 us -> none  [the longest x2 123 us: merged(): pieces = jax.tree.map(lambda part: lax.all_gather(part, axis), value)]
    div x32 -> x0, other arithmetic: 68.2 us -> none  [combine_parts(): (factor_first[..., None] * out_first + factor_second[..., None] * out_sec...]
    pallas_call x0 -> x1, Pallas kernels: none -> 50.9 us  [per_device(): pl.pallas_call(kernel, out_shape=jax.ShapeDtypeStruct((QS, columns), bf16...]
    slice x8 -> x0, local copies, waits for them, and re-layouts: 27.9 us -> none  [the longest x3 23.2 us: merged(): tail = jax.tree.map(lambda part: part[1:], pieces)]
    dot_general x17 -> x0, matrix products: 24.9 us -> none  [the longest x8 11.2 us: per_group(): lax.dot_general(query_part, key_part, (((1,), (1,)), ((), ())), preferred...]
    dynamic_update_slice x16 -> x0, local copies, waits for them, and re-layouts: 5.42 us -> none  [the longest x8 2.71 us: per_group(): maxima = lax.dynamic_update_slice_in_dim(maxima, row_max, head_start, 1)]
  transfers between devices with their start and end apart: 2 -> 0, of which waited for: 2 -> 0; matrix products, arithmetic and copies ran while one was open for 0% -> 0% of each run, Pallas kernels for 0% -> 0%
where the time goes in v1:
time: 53.7 us; the launch traced here: 53.6 us
  Pallas kernels  50.9 us (95%)
  local copies, waits for them, and re-layouts  1.32 us (2%)
  between operations  1.3 us (2%)
    pallas_call x1, Pallas kernels, per_device(): pl.pallas_call(kernel, out_shape=jax.ShapeDtypeStruct((QS, columns), bf16...  50.9 us
    unnamed x1, local copies, waits for them, and re-layouts  1.32 us

profile of v1, /device:TPU:1, one launch (start us, length us, event | category | flops | bytes accessed | tf_op | source)
XLA Modules:
  0.0 53.6 jit_solution(1576036485117809141)
XLA Ops:
  1.3 50.9 %section_attention.1 = bf16[32,256]{1,0:T(8,128)(2,1)} custom-call(s32[1]{0:T(128)S(6)} %copy.7.offsets, s32[1]{0:T(128)S(6)} %copy.8.starts, bf16[1,8192]{1,0:T(2,128)(2,1)} %q_hbm.1, bf16[2048,2048]{1,0:T(8,128)(2,1)} %cache_hbm.1, bf16[8192,256]{1,0:T(8,128)(2,1)} %w_hbm.1), custom_call_target="tpu_custom_call" | custom-call | tf_op jit(solution)/shard_map/section_attention/pallas_call | solution.py:275
  52.2 1.3 %copy.9 = bf16[32,256]{1,0:T(8,128)(2,1)} copy(bf16[32,256]{1,0:T(8,128)(2,1)} %section_attention.1) | data formatting | bytes 32768

commit v2 on v1

v2 whole, which is shorter than its diff:
```python
import functools

import jax
import jax.numpy as jnp
from jax import lax
from jax.experimental import pallas as pl
from jax.experimental.pallas import tpu as pltpu
from jax.sharding import PartitionSpec as P

VMEM_LIMIT = 40 * 1024 * 1024
H = 64
KVH = 8
HD = 128
GROUP = H // KVH
NX = 4
NZ = 8
QS = NX * NZ
ROWS = QS * GROUP
CHUNK = ROWS // NX
SCALE2 = HD ** (-0.5) * 1.4426950408889634
HIDDEN = -1e30
MESH = pl.DeviceIdType.MESH
FAR_FIRST = (4, 3, -3, 2, -2, 1, -1, 0)
Z_NEAR = (6, 5)
Z_FAR = (4, 3, 2, 1, 0)
FIRST_AT, FIRST_N, FIRST_HEADS = 3, 2, (1, 0)
REST_AT, REST_N, REST_HEADS = 5, 6, (2, 4, 6, 7, 5, 3)
SEND_AFTER = {3: (0, 1), 5: (2, 3), 7: (4, 5), 8: (6,), 9: (7,)}
JOIN_AFTER = {8: (0,), 9: (1, 2, 3, 4, 5, 6, 7)}


def kernel(off_hbm, start_hbm, q_hbm, cache_hbm, w_hbm, out_ref, off_smem, start_smem, qrow, qf,
           qdup, first_q, rest_q, qg, qb, hide, fbuf, kbuf, vbuf, wbuf, s_even, s_odd, p_even,
           p_odd, partial, osend, ostat, xbuf, xstat, zsend, zsstat, zbuf, zstat, abuf, ysend, small_load,
           q_load, k_load, v_load, w_load, fz_s, fz_r, fx_s, fx_r, rz_s, rz_r, rx_s, rx_r, xs_s,
           xs_r, zs_s, zs_r, az_s, az_r, ax_s, ax_r, y_s, y_r):
    segment = lax.axis_index("segment")
    ctx = lax.axis_index("ctx")
    z = ctx // NX
    x = ctx % NX
    n_seg = lax.axis_size("segment")
    span = cache_hbm.shape[0]
    bf16, f32 = jnp.bfloat16, jnp.float32

    def at_z(step):
        return (z + step + NZ) % NZ

    def at_x(step):
        return (x + step + NX) % NX

    def peer(zz, xx):
        return {"segment": segment, "ctx": zz * NX + xx}

    barrier = pltpu.get_barrier_semaphore()
    for step in range(1, NZ):
        pl.semaphore_signal(barrier, inc=1, device_id=peer(at_z(step), x), device_id_type=MESH)
    for step in range(1, NX):
        pl.semaphore_signal(barrier, inc=1, device_id=peer(z, at_x(step)), device_id_type=MESH)
    before = (segment + n_seg - 1) % n_seg
    after = (segment + 1) % n_seg
    pl.semaphore_signal(
        barrier, inc=1, device_id={"segment": before, "ctx": ctx}, device_id_type=MESH
    )

    q_copy = pltpu.make_async_copy(q_hbm, qrow, q_load)
    q_copy.start()
    off_copy = pltpu.make_async_copy(off_hbm, off_smem, small_load.at[0])
    start_copy = pltpu.make_async_copy(start_hbm, start_smem, small_load.at[1])
    off_copy.start()
    start_copy.start()
    k_copies, v_copies = [], []
    for k, dz in enumerate(FAR_FIRST):
        g = at_z(dz)
        k_copies.append(pltpu.make_async_copy(
            cache_hbm.at[:, pl.ds(pl.multiple_of(g * HD, HD), HD)], kbuf.at[k], k_load.at[k]))
        v_copies.append(pltpu.make_async_copy(
            cache_hbm.at[:, pl.ds(pl.multiple_of((KVH + g) * HD, HD), HD)], vbuf.at[k], v_load.at[k]))
        k_copies[k].start()
        v_copies[k].start()
    w_copy = pltpu.make_async_copy(w_hbm, wbuf, w_load)
    w_copy.start()

    q_copy.wait()
    row = qrow[...].astype(f32)
    for h in range(H):
        qf[h:h + 1, :] = row[:, h * HD:(h + 1) * HD]
    for slab in range(qdup.shape[0]):
        g = slab % KVH
        qdup[slab] = qf[g * GROUP:(g + 1) * GROUP, :].astype(bf16)
    first_q[ctx] = qdup[pl.ds(z + FIRST_AT, FIRST_N)]
    rest_q[ctx] = qdup[pl.ds(z + REST_AT, REST_N)]

    off_copy.wait()
    start_copy.wait()
    offset = off_smem[0]
    start = start_smem[0]
    first = ctx * span
    eighth = span // 8
    lanes = lax.broadcasted_iota(jnp.int32, (eighth, HD), 1)
    for part in range(8):
        position = first + part * eighth + lax.broadcasted_iota(jnp.int32, (eighth, HD), 0)
        late = jnp.clip(position - offset, 0, QS)
        late = jnp.where(position < start, QS, late)
        fbuf[part * eighth:(part + 1) * eighth, :] = jnp.where(late == lanes, 1.0, 0.0).astype(bf16)
    g_lane = lax.broadcasted_iota(jnp.int32, (ROWS, HD), 1)
    g_row = lax.broadcasted_iota(jnp.int32, (ROWS, HD), 0) % QS
    hide[...] = jnp.where((g_lane > g_row) & (g_lane <= QS), HIDDEN, 0.0).astype(bf16)

    pl.semaphore_wait(barrier, NZ - 1 + NX - 1 + 1)

    def source(i):
        return at_z(-FAR_FIRST[i])

    def two_stage(buf, z_source, z_send, z_recv, x_send, x_recv):
        def along_z(i):
            to = at_z(FAR_FIRST[i])
            return pltpu.make_async_remote_copy(
                z_source(to), buf.at[ctx], z_send.at[i], z_recv.at[i],
                device_id=peer(to, x), device_id_type=MESH)

        def along_x(i, dx):
            own = source(i) * NX + x
            return pltpu.make_async_remote_copy(
                buf.at[own], buf.at[own], x_send.at[i, dx - 1], x_recv.at[i, dx - 1],
                device_id=peer(z, at_x(dx)), device_id_type=MESH)

        def send_own():
            for i in range(NZ - 1):
                along_z(i).start()
            for dx in (2, 1, 3):
                along_x(NZ - 1, dx).start()

        def relay(i):
            along_z(i).wait_recv()
            for dx in (2, 1, 3):
                along_x(i, dx).start()

        def finish():
            for i in range(NZ - 1):
                along_z(i).wait_send()
            for i in range(NZ):
                for dx in range(1, NX):
                    along_x(i, dx).wait_send()

        return send_own, relay, lambda i, dx: along_x(i, dx).wait_recv(), finish

    send_first, relay_first, arrived_first, finish_first = two_stage(
        first_q, lambda to: qdup.at[pl.ds(to + FIRST_AT, FIRST_N)], fz_s, fz_r, fx_s, fx_r)
    send_rest, relay_rest, arrived_rest, finish_rest = two_stage(
        rest_q, lambda to: qdup.at[pl.ds(to + REST_AT, REST_N)], rz_s, rz_r, rx_s, rx_r)

    def unpack(buf, c, heads):
        for j, k in enumerate(heads):
            qg[k, pl.ds(c, GROUP, stride=QS), :] = buf[c, j].astype(f32)

    def take_first(c):
        unpack(first_q, c, FIRST_HEADS)

    def take_rest(c):
        unpack(rest_q, c, REST_HEADS)

    send_first()
    send_rest()
    take_first(ctx)
    take_rest(ctx)
    near_first = list(reversed(range(NZ - 1)))
    lag = 2
    for n in range(NZ - 1 + lag):
        if n < NZ - 1:
            relay_first(near_first[n])
            take_first(source(near_first[n]) * NX + x)
        if n >= lag:
            relay_rest(near_first[n - lag])
            take_rest(source(near_first[n - lag]) * NX + x)
    for i in reversed(range(NZ)):
        for dx in range(1, NX):
            arrived_first(i, dx)
            take_first(source(i) * NX + at_x(-dx))
    for k in FIRST_HEADS:
        qb[k] = qg[k].astype(bf16)

    def wait_rest():
        for i in reversed(range(NZ)):
            for dx in range(1, NX):
                arrived_rest(i, dx)
                take_rest(source(i) * NX + at_x(-dx))
        for k in REST_HEADS:
            qb[k] = qg[k].astype(bf16)

    lane = lax.broadcasted_iota(jnp.int32, (CHUNK, HD), 1)
    line = lax.broadcasted_iota(jnp.int32, (CHUNK, HD), 0)
    diagonal = lane == line
    diagonal_high = lane == line + CHUNK
    low = lax.broadcasted_iota(jnp.int32, (1, HD), 1) < CHUNK

    def x_copies(k, dx):
        to = at_x(dx)
        where = peer(z, to)
        return (
            pltpu.make_async_remote_copy(
                osend.at[k, pl.ds(pl.multiple_of(to * CHUNK, CHUNK), CHUNK), :],
                xbuf.at[k, dx - 1], xs_s.at[k, dx - 1, 0], xs_r.at[k, dx - 1, 0],
                device_id=where, device_id_type=MESH),
            pltpu.make_async_remote_copy(
                ostat.at[k, to, pl.ds(0, 1), :], xstat.at[k, dx - 1, pl.ds(0, 1), :],
                xs_s.at[k, dx - 1, 1], xs_r.at[k, dx - 1, 1],
                device_id=where, device_id_type=MESH),
        )

    def z_copies(k, dz):
        where = peer(at_z(dz), x)
        return (
            pltpu.make_async_remote_copy(
                zsend.at[k], zbuf.at[k], zs_s.at[k, 0], zs_r.at[k, 0],
                device_id=where, device_id_type=MESH),
            pltpu.make_async_remote_copy(
                zsstat.at[k, pl.ds(0, 1), :], zstat.at[k, pl.ds(0, 1), :],
                zs_s.at[k, 1], zs_r.at[k, 1], device_id=where, device_id_type=MESH),
        )

    def join(parts):
        top = functools.reduce(jnp.maximum, [stat for stat, _ in parts])
        total = jnp.zeros_like(top)
        mixed = jnp.zeros((CHUNK, HD), f32)
        for stat, numerator in parts:
            factor = jnp.exp2(stat - top)
            total = total + pltpu.roll(factor, CHUNK, 1) * stat
            column = jnp.sum(
                jnp.where(diagonal, jnp.broadcast_to(factor, (CHUNK, HD)), 0.0),
                axis=1, keepdims=True)
            mixed = mixed + column * numerator.astype(f32)
        return jnp.where(low, top, total), mixed

    own_rows = pl.ds(pl.multiple_of(x * CHUNK, CHUNK), CHUNK)

    def join_x(k):
        parts = [(ostat[k, x, 0:1, :], osend[k, own_rows, :])]
        for dx in range(1, NX):
            for copy in x_copies(k, dx):
                copy.wait_recv()
            parts.append((xstat[k, dx - 1, 0:1, :], xbuf[k, dx - 1]))
        stat, mixed = join(parts)
        zsend[k] = mixed.astype(bf16)
        zsstat[k, 0:1, :] = stat
        if FAR_FIRST[k] != 0:
            for copy in z_copies(k, FAR_FIRST[k]):
                copy.start()

    scores = (s_even, s_odd)
    rounded = (p_even, p_odd)
    tile, block = 256, 16
    per = CHUNK // block
    b_lane = lax.broadcasted_iota(jnp.int32, (block, HD), 1)
    b_line = lax.broadcasted_iota(jnp.int32, (block, HD), 0)

    def score_tile(k, c):
        rows = slice(c * tile, (c + 1) * tile)
        query = jnp.concatenate([qb[k], hide[...]], axis=1)
        keys = jnp.concatenate([kbuf[k, rows, :], fbuf[rows, :]], axis=1)
        scores[k % 2][:, rows] = lax.dot_general(
            query, keys, (((1,), (1,)), ((), ())), preferred_element_type=f32)

    def soften(k, r, stat):
        rows = slice(r * block, (r + 1) * block)
        score = scores[k % 2][rows, :]
        top = jnp.max(score, axis=1, keepdims=True)
        weight = jnp.exp2((score - top) * SCALE2)
        total = jnp.sum(weight, axis=1, keepdims=True)
        rounded[k % 2][rows, :] = weight.astype(bf16)
        at = b_lane - b_line - (r % per) * block
        part = jnp.where(at == 0, top * SCALE2, 0.0) + jnp.where(at == CHUNK, total, 0.0)
        part = part[:8] + part[8:]
        stat = part if r % per == 0 else stat + part
        if r % per == per - 1:
            ostat[k, r // per, 0:1, :] = jnp.sum(stat, axis=0, keepdims=True)
        return stat

    def value_tile(k, c):
        rows = slice(c * tile, (c + 1) * tile)
        term = jnp.dot(rounded[k % 2][:, rows], vbuf[k, rows, :], preferred_element_type=f32)
        if c == 0:
            partial[k % 2] = term
        elif c < tiles - 1:
            partial[k % 2] = partial[k % 2] + term
        else:
            osend[k] = (partial[k % 2] + term).astype(bf16)

    tiles = span // tile
    for k in range(KVH):
        k_copies[k].wait()
        v_copies[k].wait()
    for i in range(KVH + 2):
        if i == FIRST_N:
            wait_rest()
        stat = None
        for r in range(ROWS // block):
            if 1 <= i <= KVH:
                stat = soften(i - 1, r, stat)
            if r % 2 == 0 and i < KVH:
                score_tile(i, r // 2)
            if r % 2 == 1 and i >= 2:
                value_tile(i - 2, r // 2)
        for k in SEND_AFTER.get(i, ()):
            for dx in (2, 1, 3):
                for copy in x_copies(k, dx):
                    copy.start()
        for k in JOIN_AFTER.get(i, ()):
            join_x(k)

    own = NZ - 1
    parts = [(zsstat[own, 0:1, :], zsend[own])]
    for k in range(NZ - 1):
        for copy in z_copies(k, FAR_FIRST[k]):
            copy.wait_recv()
        parts.append((zstat[k, 0:1, :], zbuf[k]))
    stat, mixed = join(parts)
    divisor = jnp.sum(
        jnp.where(diagonal_high, jnp.broadcast_to(stat, (CHUNK, HD)), 0.0), axis=1, keepdims=True)
    mixed = mixed / divisor
    abuf[ctx] = jnp.concatenate([mixed[:QS], mixed[QS:]], axis=1).astype(bf16)

    def chunk_copy(c, send, recv, where):
        return pltpu.make_async_remote_copy(
            abuf.at[c], abuf.at[c], send, recv, device_id=where, device_id_type=MESH)

    def a_z(i):
        return chunk_copy(ctx, az_s.at[i], az_r.at[i], peer(at_z(FAR_FIRST[i]), x))

    def a_x(i, dx):
        return chunk_copy(
            source(i) * NX + x, ax_s.at[i, dx - 1], ax_r.at[i, dx - 1], peer(z, at_x(dx)))

    def a_near(i, dx):
        return chunk_copy(
            z * NX + at_x(-dx), ax_s.at[i, dx - 1], ax_r.at[i, dx - 1],
            peer(at_z(FAR_FIRST[i]), x))

    def term(c):
        return jnp.dot(
            abuf[c], wbuf[pl.ds(pl.multiple_of(c * 2 * HD, 2 * HD), 2 * HD), :],
            preferred_element_type=f32)

    mine = NZ - 1
    for i in range(mine):
        a_z(i).start()
    for dx in (2, 1, 3):
        a_x(mine, dx).start()
    w_copy.wait()
    projected = term(ctx)
    for dx in (1, 3, 2):
        a_x(mine, dx).wait_recv()
        for i in Z_NEAR:
            a_near(i, dx).start()
        projected = projected + term(z * NX + at_x(-dx))
    for i in Z_FAR:
        a_z(i).wait_recv()
        for dx in (2, 1, 3):
            a_x(i, dx).start()
        projected = projected + term(source(i) * NX + x)
    for i in Z_NEAR:
        a_z(i).wait_recv()
        projected = projected + term(source(i) * NX + x)
        for dx in (1, 3, 2):
            a_near(i, dx).wait_recv()
            projected = projected + term(source(i) * NX + at_x(-dx))
    for i in Z_FAR:
        for dx in (1, 3, 2):
            a_x(i, dx).wait_recv()
            projected = projected + term(source(i) * NX + at_x(-dx))

    def finish_a():
        for i in range(mine):
            a_z(i).wait_send()
            for dx in range(1, NX):
                (a_near if i in Z_NEAR else a_x)(i, dx).wait_send()
        for dx in range(1, NX):
            a_x(mine, dx).wait_send()

    ysend[...] = projected.astype(bf16)
    y_copy = pltpu.make_async_remote_copy(
        ysend, out_ref, y_s.at[0], y_r.at[0],
        device_id={"segment": after, "ctx": ctx}, device_id_type=MESH)
    y_copy.start()
    finish_first()
    finish_rest()
    finish_a()
    for k, dz in enumerate(FAR_FIRST):
        for dx in range(1, NX):
            for copy in x_copies(k, dx):
                copy.wait_send()
        if dz != 0:
            for copy in z_copies(k, dz):
                copy.wait_send()
    y_copy.wait()


def per_device(queries, cache, out_weight, offsets, starts):
    span = cache.shape[0]
    columns = out_weight.shape[1]
    bf16, f32 = jnp.bfloat16, jnp.float32
    dma = pltpu.SemaphoreType.DMA
    hop = [dma((NZ - 1,)), dma((NZ - 1,)), dma((NZ, NX - 1)), dma((NZ, NX - 1))]
    return pl.pallas_call(
        kernel,
        out_shape=jax.ShapeDtypeStruct((QS, columns), bf16),
        in_specs=[pl.BlockSpec(memory_space=pltpu.HBM)] * 5,
        out_specs=pl.BlockSpec(memory_space=pltpu.VMEM),
        scratch_shapes=[
            pltpu.SMEM((1,), jnp.int32),
            pltpu.SMEM((1,), jnp.int32),
            pltpu.VMEM((1, H * HD), bf16),
            pltpu.VMEM((H, HD), f32),
            pltpu.VMEM((REST_AT + REST_N + NZ - 1, GROUP, HD), bf16),
            pltpu.VMEM((QS, FIRST_N, GROUP, HD), bf16),
            pltpu.VMEM((QS, REST_N, GROUP, HD), bf16),
            pltpu.VMEM((KVH, ROWS, HD), f32),
            pltpu.VMEM((KVH, ROWS, HD), bf16),
            pltpu.VMEM((ROWS, HD), bf16),
            pltpu.VMEM((span, HD), bf16),
            pltpu.VMEM((KVH, span, HD), bf16),
            pltpu.VMEM((KVH, span, HD), bf16),
            pltpu.VMEM((H * HD, columns), bf16),
            pltpu.VMEM((ROWS, span), f32),
            pltpu.VMEM((ROWS, span), f32),
            pltpu.VMEM((ROWS, span), bf16),
            pltpu.VMEM((ROWS, span), bf16),
            pltpu.VMEM((2, ROWS, HD), f32),
            pltpu.VMEM((KVH, ROWS, HD), bf16),
            pltpu.VMEM((KVH, NX, 8, HD), f32),
            pltpu.VMEM((KVH, NX - 1, CHUNK, HD), bf16),
            pltpu.VMEM((KVH, NX - 1, 8, HD), f32),
            pltpu.VMEM((NZ, CHUNK, HD), bf16),
            pltpu.VMEM((NZ, 8, HD), f32),
            pltpu.VMEM((NZ, CHUNK, HD), bf16),
            pltpu.VMEM((NZ, 8, HD), f32),
            pltpu.VMEM((QS, QS, 2 * HD), bf16),
            pltpu.VMEM((QS, columns), bf16),
            dma((2,)), dma, dma((KVH,)), dma((KVH,)), dma,
            *hop, *hop,
            dma((KVH, NX - 1, 2)), dma((KVH, NX - 1, 2)),
            dma((NZ - 1, 2)), dma((NZ - 1, 2)),
            *hop,
            dma((1,)), dma((1,)),
        ],
        compiler_params=pltpu.CompilerParams(collective_id=0, has_side_effects=True, vmem_limit_bytes=VMEM_LIMIT),
        name="section_attention",
    )(offsets, starts, *[
        pltpu.with_memory_space_constraint(a, pltpu.HBM) for a in (queries, cache, out_weight)])


def solution(mesh):
    in_specs = (
        P(("segment", "ctx"), None),
        P(("segment", "ctx"), None),
        P("segment", "ctx"),
        P("segment"),
        P("segment"),
    )
    out_specs = P("segment", "ctx")
    return jax.shard_map(
        per_device, mesh=mesh, in_specs=in_specs, out_specs=out_specs, check_vma=False
    )
```

time: 53.7 us -> 50.7 us (0.944)
  Pallas kernels: 50.9 us -> 48.7 us
  local copies, waits for them, and re-layouts: 1.32 us -> 0.61 us
    pallas_call x1, Pallas kernels: 50.9 us -> 48.7 us  [per_device(): pl.pallas_call(kernel, out_shape=jax.ShapeDtypeStruct((QS, columns), bf16...]
    unnamed x1, local copies, waits for them, and re-layouts: 1.32 us -> 0.61 us
where the time goes in v2:
time: 50.7 us; the launch traced here: 50.6 us
  Pallas kernels  48.7 us (96%)
  between operations  1.3 us (3%)
  local copies, waits for them, and re-layouts  0.61 us (1%)
    pallas_call x1, Pallas kernels, per_device(): pl.pallas_call(kernel, out_shape=jax.ShapeDtypeStruct((QS, columns), bf16...  48.7 us

profile of v2, /device:TPU:1, one launch (start us, length us, event | category | flops | bytes accessed | tf_op | source)
XLA Modules:
  0.0 50.6 jit_solution(4131510384267275720)
XLA Ops:
  1.3 48.7 %section_attention.1 = bf16[32,256]{1,0:T(8,128)(2,1)S(1)} custom-call(s32[1]{0:T(128)S(6)} %copy.7.off_hbm, s32[1]{0:T(128)S(6)} %copy.8.start_hbm, bf16[1,8192]{1,0:T(2,128)(2,1)} %q_hbm.1, bf16[2048,2048]{1,0:T(8,128)(2,1)} %cache_hbm.1, bf16[8192,256]{1,0:T(8,128)(2,1)} %w_hbm.1), custom_call_target="tpu_custom_call" | custom-call | tf_op jit(solution)/shard_map/section_attention/pallas_call | solution.py:403
  50.0 0.6 %copy.9 = bf16[32,256]{1,0:T(8,128)(2,1)} copy(bf16[32,256]{1,0:T(8,128)(2,1)S(1)} %section_attention.1) | data formatting | bytes 32768

commit v3 on v2

--- a/solution.py
+++ b/solution.py
@@ -25,8 +25,8 @@
 Z_FAR = (4, 3, 2, 1, 0)
 FIRST_AT, FIRST_N, FIRST_HEADS = 3, 2, (1, 0)
 REST_AT, REST_N, REST_HEADS = 5, 6, (2, 4, 6, 7, 5, 3)
-SEND_AFTER = {3: (0, 1), 5: (2, 3), 7: (4, 5), 8: (6,), 9: (7,)}
-JOIN_AFTER = {8: (0,), 9: (1, 2, 3, 4, 5, 6, 7)}
+SEND_AFTER = {3: (0, 1), 5: (2, 3), 7: (4, 5), 9: (6, 7)}
+JOIN_AFTER = {9: (0, 1, 2, 3, 4, 5, 6, 7)}
 
 
 def kernel(off_hbm, start_hbm, q_hbm, cache_hbm, w_hbm, out_ref, off_smem, start_smem, qrow, qf,
@@ -164,7 +164,7 @@
     take_first(ctx)
     take_rest(ctx)
     near_first = list(reversed(range(NZ - 1)))
-    lag = 2
+    lag = 7
     for n in range(NZ - 1 + lag):
         if n < NZ - 1:
             relay_first(near_first[n])

time: 50.7 us -> 48.9 us (0.964)
  Pallas kernels: 48.7 us -> 46.9 us
    pallas_call x1, Pallas kernels: 48.7 us -> 46.9 us  [per_device(): pl.pallas_call(kernel, out_shape=jax.ShapeDtypeStruct((QS, columns), bf16...]
where the time goes in v3:
time: 48.9 us; the launch traced here: 48.8 us
  Pallas kernels  46.9 us (96%)
  between operations  1.3 us (3%)
  local copies, waits for them, and re-layouts  0.61 us (1%)
    pallas_call x1, Pallas kernels, per_device(): pl.pallas_call(kernel, out_shape=jax.ShapeDtypeStruct((QS, columns), bf16...  46.9 us

profile of v3, /device:TPU:1, one launch (start us, length us, event | category | flops | bytes accessed | tf_op | source)
XLA Modules:
  0.0 48.8 jit_solution(7136141176106124781)
XLA Ops:
  1.3 46.9 %section_attention.1 = bf16[32,256]{1,0:T(8,128)(2,1)S(1)} custom-call(s32[1]{0:T(128)S(6)} %copy.7.off_hbm, s32[1]{0:T(128)S(6)} %copy.8.start_hbm, bf16[1,8192]{1,0:T(2,128)(2,1)} %q_hbm.1, bf16[2048,2048]{1,0:T(8,128)(2,1)} %cache_hbm.1, bf16[8192,256]{1,0:T(8,128)(2,1)} %w_hbm.1), custom_call_target="tpu_custom_call" | custom-call | tf_op jit(solution)/shard_map/section_attention/pallas_call | solution.py:403
  48.2 0.6 %copy.9 = bf16[32,256]{1,0:T(8,128)(2,1)} copy(bf16[32,256]{1,0:T(8,128)(2,1)S(1)} %section_attention.1) | data formatting | bytes 32768

commit v4 on v3

--- a/solution.py
+++ b/solution.py
@@ -168,10 +168,12 @@
     for n in range(NZ - 1 + lag):
         if n < NZ - 1:
             relay_first(near_first[n])
-            take_first(source(near_first[n]) * NX + x)
         if n >= lag:
             relay_rest(near_first[n - lag])
-            take_rest(source(near_first[n - lag]) * NX + x)
+    for i in near_first:
+        take_first(source(i) * NX + x)
+    for i in near_first:
+        take_rest(source(i) * NX + x)
     for i in reversed(range(NZ)):
         for dx in range(1, NX):
             arrived_first(i, dx)
@@ -335,9 +337,11 @@
             z * NX + at_x(-dx), ax_s.at[i, dx - 1], ax_r.at[i, dx - 1],
             peer(at_z(FAR_FIRST[i]), x))
 
-    def term(c):
+    def term(row):
+        chunks = jnp.concatenate([abuf[row * NX + xx] for xx in range(NX)], axis=1)
+        depth = NX * 2 * HD
         return jnp.dot(
-            abuf[c], wbuf[pl.ds(pl.multiple_of(c * 2 * HD, 2 * HD), 2 * HD), :],
+            chunks, wbuf[pl.ds(pl.multiple_of(row * depth, depth), depth), :],
             preferred_element_type=f32)
 
     mine = NZ - 1
@@ -345,28 +349,25 @@
         a_z(i).start()
     for dx in (2, 1, 3):
         a_x(mine, dx).start()
-    w_copy.wait()
-    projected = term(ctx)
     for dx in (1, 3, 2):
         a_x(mine, dx).wait_recv()
         for i in Z_NEAR:
             a_near(i, dx).start()
-        projected = projected + term(z * NX + at_x(-dx))
     for i in Z_FAR:
         a_z(i).wait_recv()
         for dx in (2, 1, 3):
             a_x(i, dx).start()
-        projected = projected + term(source(i) * NX + x)
+    w_copy.wait()
+    projected = term(z)
     for i in Z_NEAR:
         a_z(i).wait_recv()
-        projected = projected + term(source(i) * NX + x)
         for dx in (1, 3, 2):
             a_near(i, dx).wait_recv()
-            projected = projected + term(source(i) * NX + at_x(-dx))
+        projected = projected + term(source(i))
     for i in Z_FAR:
         for dx in (1, 3, 2):
             a_x(i, dx).wait_recv()
-            projected = projected + term(source(i) * NX + at_x(-dx))
+        projected = projected + term(source(i))
 
     def finish_a():
         for i in range(mine):

time: 48.9 us -> 49 us (level)
  no operation moved by 1% of the time
where the time goes in v4:
time: 49 us; the launch traced here: 48.9 us
  Pallas kernels  47 us (96%)
  between operations  1.3 us (3%)
  local copies, waits for them, and re-layouts  0.61 us (1%)
    pallas_call x1, Pallas kernels, per_device(): pl.pallas_call(kernel, out_shape=jax.ShapeDtypeStruct((QS, columns), bf16...  47 us

profile of v4, /device:TPU:1, one launch (start us, length us, event | category | flops | bytes accessed | tf_op | source)
XLA Modules:
  0.0 48.9 jit_solution(6966036571129142542)
XLA Ops:
  1.3 47.0 %section_attention.1 = bf16[32,256]{1,0:T(8,128)(2,1)S(1)} custom-call(s32[1]{0:T(128)S(6)} %copy.7.off_hbm, s32[1]{0:T(128)S(6)} %copy.8.start_hbm, bf16[1,8192]{1,0:T(2,128)(2,1)} %q_hbm.1, bf16[2048,2048]{1,0:T(8,128)(2,1)} %cache_hbm.1, bf16[8192,256]{1,0:T(8,128)(2,1)} %w_hbm.1), custom_call_target="tpu_custom_call" | custom-call | tf_op jit(solution)/shard_map/section_attention/pallas_call | solution.py:404
  48.3 0.6 %copy.9 = bf16[32,256]{1,0:T(8,128)(2,1)} copy(bf16[32,256]{1,0:T(8,128)(2,1)S(1)} %section_attention.1) | data formatting | bytes 32768
